TPU v7x, 32 devices: a whole 2x2x4 slice. The times are simulated.
32 devices in a mesh: dp: 8 (over z, y), seq: 4 (over x, core).
Axes of the slice: x: 2, y: 2, z: 4, core: 2. Of those that a mesh axis runs over, the one named last changes fastest.
Arguments:
- tokens: bfloat16 [8, 512, 768], P('dp', 'seq'), may hold values from -6 to 6
- cotangent: bfloat16 [8, 512, 768], P('dp', 'seq'), may hold values from -6 to 6
- segment_ids: int32 [8, 512], P('dp', 'seq'), may hold values from 0 to 7, never falling along the last dimension, each value on 1 to 256 neighbouring positions
- pad_mask: int32 [8, 512], P('dp', 'seq'), may hold values 0 or 1
- routes: int32 [8, 512, 2], P('dp', 'seq'), may hold values from 0 to 3, all different within a row; in each aligned block of 128 rows (0 to 127, 128 to 255, ..., all dimensions but the last counted through in order) at most 96 rows name the same one
- gate_weights: float32 [8, 512, 2], P('dp', 'seq'), may hold values from 0.25 to 1
- gain_one: float32 [768], replicated, may hold values from 0.5 to 1.5
- w_qkv: bfloat16 [768, 2304], P(('dp', 'seq')), may hold values from -0.21875 to 0.21875
- w_attn: bfloat16 [768, 768], P(('dp', 'seq')), may hold values from -1.75 to 1.75
- rel_table: bfloat16 [12, 32], replicated, may hold values from -4 to 4
- gain_two: float32 [768], replicated, may hold values from 0.5 to 1.5
- w_expert_in: bfloat16 [4, 768, 3072], P(None, ('dp', 'seq')), may hold values from -0.21875 to 0.21875
- w_expert_out: bfloat16 [4, 3072, 768], P(None, ('dp', 'seq')), may hold values from -0.109375 to 0.109375
Outputs:
- output: bfloat16 [8, 512, 768], P('dp', 'seq')
- grad_tokens: float32 [8, 512, 768], P('dp', 'seq')
- grad_gain_one: float32 [768], replicated
- grad_w_qkv: float32 [768, 2304], P(('dp', 'seq'))
- grad_w_attn: float32 [768, 768], P(('dp', 'seq'))
- grad_rel_table: float32 [12, 32], replicated
- grad_gain_two: float32 [768], replicated
- grad_expert_in: float32 [4, 768, 3072], P(None, ('dp', 'seq'))
- grad_expert_out: float32 [4, 3072, 768], P(None, ('dp', 'seq'))
Inputs may be any that keep to these rules, and one draw needn't show every extreme that they name: `routes`: the two experts of a token differ. Among the rows of one device no expert is named more than 96 times, and in some device's rows one expert is named exactly 96 times. `segment_ids`: ids never fall along a sequence; a document has 1 to 256 positions, and one has exactly that many.
All inputs are finite; a program needn't handle non-finite values. No bound on the sum of `pad_mask` on one device may be relied on, other than what follows from the above.
Results may differ from a plain program's by a relative error of at most 0.011.
Values may be sent and summed in bfloat16 or wider, within the bound.
No kernel may reach another device: no remote copies, remote signals or barrier semaphores. Data moves between devices by JAX's collectives and lax.ppermute only.
A program may use at most 320 MiB of HBM per device.

v0:
```python
import math
import jax
import jax.numpy as jnp
import numpy as np
from jax import lax
from jax.sharding import PartitionSpec as P

BUCKETS = 32
MAX_DIST = 128
CAP = 96


def bucket_edges():
    exact_span = BUCKETS // 2
    distance = np.arange(1, 8 * MAX_DIST + 1)
    widened = np.maximum(distance, exact_span) / exact_span
    spread = exact_span + (np.log(widened) / np.log(MAX_DIST / exact_span) * exact_span).astype(
        np.int64
    )
    bucket_of = np.where(distance < exact_span, distance, np.minimum(spread, BUCKETS - 1))
    return np.array(
        [distance[np.argmax(bucket_of >= target)] for target in range(1, BUCKETS)], dtype=np.int32
    )


def norm_stats(values):
    factor = lax.rsqrt(jnp.mean(values * values, axis=-1, keepdims=True) + 1e-06)
    return (values * factor, factor)


def norm_back(grad_normed, scaled, factor, gain_vec):
    grad_scaled = grad_normed * gain_vec
    inner_mean = jnp.mean(grad_scaled * scaled, axis=-1, keepdims=True)
    return (factor * (grad_scaled - scaled * inner_mean), jnp.sum(grad_normed * scaled, axis=0))


def make_onehot(distance, edges_np):
    bucket_of = jnp.sum((distance[:, :, None] >= edges_np).astype(jnp.int32), axis=-1)
    return (bucket_of[:, :, None] == jnp.arange(BUCKETS, dtype=jnp.int32)).astype(jnp.bfloat16)


def block_bias(table_low, edges_np, distance):
    far_away = jnp.min(distance) >= int(edges_np[-1])

    def block_detailed(unused):
        return jnp.einsum(
            "qkb,hb->hqk",
            make_onehot(distance, edges_np),
            table_low,
            preferred_element_type=jnp.float32,
        )

    def block_constant(unused):
        last_col = table_low[:, BUCKETS - 1].astype(jnp.float32)
        return jnp.broadcast_to(last_col[:, None, None], (table_low.shape[0],) + distance.shape)

    return lax.cond(far_away, block_constant, block_detailed, 0)


def table_part(grad_low, edges_np, distance):
    far_away = jnp.min(distance) >= int(edges_np[-1])

    def table_detailed(unused):
        return jnp.einsum(
            "hqk,qkb->hb",
            grad_low,
            make_onehot(distance, edges_np),
            preferred_element_type=jnp.float32,
        )

    def table_constant(unused):
        totals = jnp.sum(grad_low, axis=(1, 2), dtype=jnp.float32)
        return totals[:, None] * (jnp.arange(BUCKETS) == BUCKETS - 1).astype(jnp.float32)

    return lax.cond(far_away, table_constant, table_detailed, 0)


def body(
    tokens,
    cotangent,
    segment_ids,
    pad_mask,
    routes,
    gate_weights,
    gain_one,
    w_qkv,
    w_attn,
    rel_table,
    gain_two,
    w_expert_in,
    w_expert_out,
):
    gathered = (
        lax.all_gather(w_qkv, ("dp", "seq"), axis=0, tiled=True),
        lax.all_gather(w_attn, ("dp", "seq"), axis=0, tiled=True),
        lax.all_gather(w_expert_in, ("dp", "seq"), axis=1, tiled=True),
        lax.all_gather(w_expert_out, ("dp", "seq"), axis=1, tiled=True),
    )
    full_qkv, full_attn, full_in, full_out = gathered
    inputs = tokens[0].astype(jnp.float32)
    row_count, model_width = inputs.shape
    head_count = rel_table.shape[0]
    head_size = model_width // head_count
    score_scale = head_size ** (-0.5)
    seg_local = segment_ids[0]
    seq_index = lax.axis_index("seq")
    length = row_count * lax.axis_size("seq")
    key_block = math.gcd(length, 512)
    query_pos = seq_index * row_count + jnp.arange(row_count, dtype=jnp.int32)
    block_count = ((seq_index + 1) * row_count + key_block - 1) // key_block
    edges_np = bucket_edges()
    scaled_one, factor_one = norm_stats(inputs)
    normed_one = (scaled_one * gain_one).astype(jnp.bfloat16)
    project = jnp.dot(normed_one, full_qkv, preferred_element_type=jnp.float32)
    queries = project[:, :model_width].astype(jnp.bfloat16)
    keys_local = project[:, model_width : 2 * model_width].astype(jnp.bfloat16)
    values_local = project[:, 2 * model_width :].astype(jnp.bfloat16)
    info_local = jnp.where(pad_mask[0] == 1, seg_local, -1)
    keys_all, values_all, info_all, seg_all = (
        lax.all_gather(keys_local, "seq", axis=0, tiled=True),
        lax.all_gather(values_local, "seq", axis=0, tiled=True),
        lax.all_gather(info_local, "seq", axis=0, tiled=True),
        lax.all_gather(seg_local, "seq", axis=0, tiled=True),
    )
    query_heads = queries.reshape(row_count, head_count, head_size)

    def block_scores(block_index):
        key_start = block_index * key_block
        key_heads = lax.dynamic_slice_in_dim(keys_all, key_start, key_block, 0).reshape(
            key_block, head_count, head_size
        )
        value_heads = lax.dynamic_slice_in_dim(values_all, key_start, key_block, 0).reshape(
            key_block, head_count, head_size
        )
        info_block = lax.dynamic_slice_in_dim(info_all, key_start, key_block, 0)
        key_pos = key_start + jnp.arange(key_block, dtype=jnp.int32)
        distance = query_pos[:, None] - key_pos[None, :]
        allowed = (distance >= 0) & ((info_block[None, :] == seg_local[:, None]) | (distance == 0))
        raw_scores = (
            jnp.einsum("qhd,khd->hqk", query_heads, key_heads, preferred_element_type=jnp.float32)
            * score_scale
        )
        raw_scores = raw_scores + block_bias(rel_table, edges_np, distance)
        return (
            jnp.where(allowed[None], raw_scores, -1e30),
            allowed[None],
            key_heads,
            value_heads,
            distance,
            key_start,
        )

    def max_step(block_index, running):
        top_score, row_total = running
        pieces = block_scores(block_index)
        new_top = jnp.maximum(top_score, jnp.max(pieces[0], axis=-1))
        exponent = jnp.where(pieces[1], jnp.exp(pieces[0] - new_top[:, :, None]), 0.0)
        return (new_top, row_total * jnp.exp(top_score - new_top) + jnp.sum(exponent, axis=-1))

    start_top = jnp.full((head_count, row_count), -1e30, jnp.float32)
    start_total = jnp.zeros((head_count, row_count), jnp.float32)
    top_score, row_total = lax.fori_loop(0, block_count, max_step, (start_top, start_total))
    log_total = top_score + jnp.log(row_total)

    def out_step(block_index, mixed_acc):
        pieces = block_scores(block_index)
        prob_low = jnp.where(pieces[1], jnp.exp(pieces[0] - log_total[:, :, None]), 0.0).astype(
            jnp.bfloat16
        )
        return mixed_acc + jnp.einsum(
            "hqk,khd->qhd", prob_low, pieces[3], preferred_element_type=jnp.float32
        )

    mixed_full = lax.fori_loop(
        0, block_count, out_step, jnp.zeros((row_count, head_count, head_size), jnp.float32)
    )
    mixed_low = mixed_full.reshape(row_count, model_width).astype(jnp.bfloat16)
    hidden_one = inputs + jnp.dot(mixed_low, full_attn, preferred_element_type=jnp.float32)
    scaled_two, factor_two = norm_stats(hidden_one)
    normed_two = (scaled_two * gain_two).astype(jnp.bfloat16)
    route_local = routes[0]
    expert_count = w_expert_in.shape[0]
    top_count = route_local.shape[1]
    flat_routes = route_local.reshape(-1)
    expert_hot = (flat_routes[:, None] == jnp.arange(expert_count, dtype=jnp.int32)).astype(
        jnp.int32
    )
    earlier = jnp.cumsum(expert_hot, axis=0) - expert_hot
    slot_index = jnp.sum(earlier * expert_hot, axis=1)
    slot_float = (
        (slot_index[:, None] == jnp.arange(CAP, dtype=jnp.int32))
        .astype(jnp.float32)
        .reshape(row_count, top_count, CAP)
    )
    expert_float = expert_hot.astype(jnp.float32).reshape(row_count, top_count, expert_count)
    dispatch = jnp.einsum(
        "tke,tkc->ect",
        expert_float.astype(jnp.bfloat16),
        slot_float.astype(jnp.bfloat16),
        preferred_element_type=jnp.float32,
    ).astype(jnp.bfloat16)
    slot_gate = jnp.einsum(
        "tke,tkc,tk->ec", expert_float, slot_float, gate_weights[0], precision=lax.Precision.HIGHEST
    )
    entered = jnp.einsum(
        "ect,td->ecd", dispatch, normed_two, preferred_element_type=jnp.float32
    ).astype(jnp.bfloat16)
    pre_act = jnp.einsum("ecd,edf->ecf", entered, full_in, preferred_element_type=jnp.float32)
    active = jax.nn.gelu(pre_act).astype(jnp.bfloat16)
    result = jnp.einsum("ecf,efd->ecd", active, full_out, preferred_element_type=jnp.float32)
    expert_low = (slot_gate[:, :, None] * result).astype(jnp.bfloat16)
    combined = jnp.einsum("ect,ecd->td", dispatch, expert_low, preferred_element_type=jnp.float32)
    output = (hidden_one + combined).astype(jnp.bfloat16)
    regathered = (
        lax.all_gather(w_qkv, ("dp", "seq"), axis=0, tiled=True),
        lax.all_gather(w_attn, ("dp", "seq"), axis=0, tiled=True),
        lax.all_gather(w_expert_in, ("dp", "seq"), axis=1, tiled=True),
        lax.all_gather(w_expert_out, ("dp", "seq"), axis=1, tiled=True),
    )
    back_qkv, back_attn, back_in, back_out = regathered
    grad_out_low = cotangent[0]
    grad_slots = jnp.einsum(
        "ect,td->ecd", dispatch, grad_out_low, preferred_element_type=jnp.float32
    )
    grad_result = (slot_gate[:, :, None] * grad_slots).astype(jnp.bfloat16)
    grad_w_out = jnp.einsum("ecf,ecd->efd", active, grad_result, preferred_element_type=jnp.float32)
    grad_active = jnp.einsum(
        "ecd,efd->ecf", grad_result, back_out, preferred_element_type=jnp.float32
    )
    unused_value, gelu_pull = jax.vjp(jax.nn.gelu, pre_act)
    grad_pre = gelu_pull(grad_active)[0].astype(jnp.bfloat16)
    grad_w_in = jnp.einsum("ecd,ecf->edf", entered, grad_pre, preferred_element_type=jnp.float32)
    grad_entered = jnp.einsum(
        "ecf,edf->ecd", grad_pre, back_in, preferred_element_type=jnp.float32
    ).astype(jnp.bfloat16)
    grad_normed_two = jnp.einsum(
        "ect,ecd->td", dispatch, grad_entered, preferred_element_type=jnp.float32
    )
    grad_hidden_norm, grad_gain_two = norm_back(grad_normed_two, scaled_two, factor_two, gain_two)
    grad_hidden = grad_out_low.astype(jnp.float32) + grad_hidden_norm
    branch_low = grad_hidden.astype(jnp.bfloat16)
    grad_w_attn = lax.dot_general(
        mixed_low, branch_low, (((0,), (0,)), ((), ())), preferred_element_type=jnp.float32
    )
    grad_mixed = lax.dot_general(
        branch_low, back_attn, (((1,), (1,)), ((), ())), preferred_element_type=jnp.float32
    ).astype(jnp.bfloat16)
    grad_mixed_heads = grad_mixed.reshape(row_count, head_count, head_size)
    row_delta = jnp.sum(grad_mixed_heads.astype(jnp.float32) * mixed_full, axis=-1).T

    def score_grads(pieces):
        prob_full = jnp.where(pieces[1], jnp.exp(pieces[0] - log_total[:, :, None]), 0.0)
        grad_prob = jnp.einsum(
            "qhd,khd->hqk", grad_mixed_heads, pieces[3], preferred_element_type=jnp.float32
        )
        grad_score = (prob_full * (grad_prob - row_delta[:, :, None])).astype(jnp.bfloat16)
        return (prob_full.astype(jnp.bfloat16), grad_score)

    start_query = jnp.zeros((row_count, head_count, head_size), jnp.float32)
    start_table = jnp.zeros((head_count, BUCKETS), jnp.float32)

    def back_step(block_index, running):
        grad_query, grad_key_all, grad_value_all, grad_table = running
        pieces = block_scores(block_index)
        prob_low, grad_score = score_grads(pieces)
        grad_query = (
            grad_query
            + jnp.einsum("hqk,khd->qhd", grad_score, pieces[2], preferred_element_type=jnp.float32)
            * score_scale
        )
        key_part = (
            jnp.einsum("hqk,qhd->khd", grad_score, query_heads, preferred_element_type=jnp.float32)
            * score_scale
        ).reshape(key_block, model_width)
        value_part = jnp.einsum(
            "hqk,qhd->khd", prob_low, grad_mixed_heads, preferred_element_type=jnp.float32
        ).reshape(key_block, model_width)
        grad_key_all = lax.dynamic_update_slice_in_dim(grad_key_all, key_part, pieces[5], 0)
        grad_value_all = lax.dynamic_update_slice_in_dim(grad_value_all, value_part, pieces[5], 0)
        grad_table = grad_table + table_part(grad_score, edges_np, pieces[4])
        return (grad_query, grad_key_all, grad_value_all, grad_table)

    start_back = (
        start_query,
        jnp.zeros((length, model_width), jnp.float32),
        jnp.zeros((length, model_width), jnp.float32),
        start_table,
    )
    grad_query, grad_key_all, grad_value_all, grad_table = lax.fori_loop(
        0, block_count, back_step, start_back
    )
    grad_keys, grad_values = (
        lax.psum_scatter(
            grad_key_all.astype(jnp.bfloat16), "seq", scatter_dimension=0, tiled=True
        ).astype(jnp.float32),
        lax.psum_scatter(
            grad_value_all.astype(jnp.bfloat16), "seq", scatter_dimension=0, tiled=True
        ).astype(jnp.float32),
    )
    grad_proj = jnp.concatenate(
        [
            grad_query.reshape(row_count, model_width).astype(jnp.bfloat16),
            grad_keys.astype(jnp.bfloat16),
            grad_values.astype(jnp.bfloat16),
        ],
        axis=1,
    )
    grad_w_qkv = lax.dot_general(
        normed_one, grad_proj, (((0,), (0,)), ((), ())), preferred_element_type=jnp.float32
    )
    grad_normed_one = lax.dot_general(
        grad_proj, back_qkv, (((1,), (1,)), ((), ())), preferred_element_type=jnp.float32
    )
    grad_input_norm, grad_gain_one = norm_back(grad_normed_one, scaled_one, factor_one, gain_one)
    grad_inputs = grad_hidden + grad_input_norm
    table_total, gain_one_total, gain_two_total = lax.psum(
        (grad_table, grad_gain_one, grad_gain_two), ("dp", "seq")
    )
    shares = (
        lax.psum_scatter(grad_w_qkv, ("dp", "seq"), scatter_dimension=0, tiled=True),
        lax.psum_scatter(grad_w_attn, ("dp", "seq"), scatter_dimension=0, tiled=True),
        lax.psum_scatter(grad_w_in, ("dp", "seq"), scatter_dimension=1, tiled=True),
        lax.psum_scatter(grad_w_out, ("dp", "seq"), scatter_dimension=1, tiled=True),
    )
    return (
        output[None],
        grad_inputs[None],
        gain_one_total,
        shares[0],
        shares[1],
        table_total,
        gain_two_total,
        shares[2],
        shares[3],
    )


def solution(mesh):
    return jax.shard_map(
        body,
        mesh=mesh,
        in_specs=(
            P("dp", "seq", None),
            P("dp", "seq", None),
            P("dp", "seq"),
            P("dp", "seq"),
            P("dp", "seq", None),
            P("dp", "seq", None),
            P(),
            P(("dp", "seq"), None),
            P(("dp", "seq"), None),
            P(),
            P(),
            P(None, ("dp", "seq"), None),
            P(None, ("dp", "seq"), None),
        ),
        out_specs=(
            P("dp", "seq", None),
            P("dp", "seq", None),
            P(),
            P(("dp", "seq"), None),
            P(("dp", "seq"), None),
            P(),
            P(),
            P(None, ("dp", "seq"), None),
            P(None, ("dp", "seq"), None),
        ),
        check_vma=False,
    )
```

profile of v0, /device:TPU:0, one launch (start us, length us, event | category | flops | bytes accessed | tf_op | source)
XLA Modules:
  0.0 1434.7 jit_solution(6802587693438444505)
XLA Ops:
  15.2 5.9 all-gather
  23.1 2.0 fusion.47
  25.1 48.6 %all-gather.6.cloned.1.call-done = bf16[768,2304]{1,0:T(8,128)(2,1)} async-done(((bf16[24,2304]{1,0:T(8,128)(2,1)}), bf16[768,2304]{1,0:T(8,128)(2,1)}) %all-gather.6.cloned.1.call-update) | async-done | bytes 3538960 | tf_op jit(solution)/shard_map/all_gather | solution.py:94
  73.8 2.7 convolution_convert_fusion
  76.6 8.6 all_gather.27
  86.5 8.7 all_gather.28
  97.0 10.8 while.44
  98.5 4.7 conditional.20
  101.4 1.8 copy.138
  104.1 2.0 fusion.162
  108.5 12.9 while.45
  110.2 6.7 conditional.21
  110.2 1.7 convert_reduce_fusion.4
  113.2 3.6 copy.139
  117.7 3.5 fusion.167
  121.5 8.0 all-gather.8.cloned.1.call-done
  129.5 1.7 multiply_reduce_fusion.3
  132.5 123.6 %all-gather.12.cloned.1.call-done = bf16[4,3072,768]{2,1,0:T(8,128)(2,1)} async-done(((bf16[4,96,768]{2,1,0:T(8,128)(2,1)}), bf16[4,3072,768]{2,1,0:T(8,128)(2,1)}) %all-gather.12.cloned.1.call-update) | async-done | bytes 18874384 | tf_op jit(solution)/shard_map/all_gather | solution.py:97
  256.1 14.2 fusion.98
  270.3 111.4 %all-gather.10.cloned.1.call-done = bf16[4,768,3072]{2,1,0:T(8,128)(2,1)} async-done(((bf16[4,24,3072]{2,1,0:T(8,128)(2,1)}), bf16[4,768,3072]{2,1,0:T(8,128)(2,1)}) %all-gather.10.cloned.1.call-update) | async-done | bytes 18874384 | tf_op jit(solution)/shard_map/all_gather | solution.py:96
  381.7 11.7 fusion.46
  393.4 14.6 %multiply_reduce_fusion = (f32[768]{0:T(1024)}, f32[128]{0:T(128)S(1)}, f32[128,768]{1,0:T(8,128)}) fusion(f32[128,768]{1,0:T(8,128)S(1)} %get-tuple-element.749, f32[128]{0:T(128)S(1)} %add_rsqrt_fusion, f32[768]{0:T(1024)S(1)} %copy-done.44, bf16[4,96,128]{2,1,0:T(8,128)(2,1)S(1)} %copy-done.25, bf16[4,96,3072]{2,1,0:T(8,128)(2,1)S(1)} %get-tuple-element.750, ...), kind=kOutput, calls=%fused_computation.122 | convolution fusion | flops 1888320640 | bytes 22125568 | tf_op jit(solution)/shard_map/ect,ecd->td/dot_general | solution.py:236
  409.9 1.8 convolution_convert_fusion.3
  416.3 23.6 %while.46 = (s32[]{:T(128)}, f32[128,12,64]{0,2,1:T(8,128)}, bf16[512,768]{0,1:T(8,128)(2,1)}, bf16[512,768]{0,1:T(8,128)(2,1)}, f32[12,32]{1,0:T(8,128)S(1)}, /...) while((s32[]{:T(128)}, f32[128,12,64]{0,2,1:T(8,128)}, ...), condition=%wide.region_30.31_spmd.clone.clone, body=%wide.region_21.30_spmd.sunk.clone.clone.sunk | while | flops 628818944 | bytes 50517476 | solution.py:289
  418.3 4.7 conditional.22
  421.2 1.8 copy.135
  423.9 2.4 exponential_select_fusion.2
  426.3 1.7 multiply_convert_fusion.7
  430.0 2.2 fusion.180
  432.2 7.6 conditional.23
  432.2 3.0 copy.106
  436.9 2.9 fusion.15
  439.9 2.3 copy.127
  442.3 2.3 copy.125
  444.7 1.8 fusion.77
  446.9 17.0 %reduce-scatter.21.cloned.1.call-done = bf16[128,768]{1,0:T(8,128)(2,1)} async-done(((bf16[512,768]{1,0:T(8,128)(2,1)}), bf16[128,768]{1,0:T(8,128)(2,1)}) %reduce-scatter.21.cloned.1.call-update) | async-done | bytes 196624
  465.0 25.3 %reduce-scatter.19.cloned.1.call-done = bf16[128,768]{1,0:T(8,128)(2,1)} async-done(((bf16[512,768]{1,0:T(8,128)(2,1)}), bf16[128,768]{1,0:T(8,128)(2,1)}) %reduce-scatter.19.cloned.1.call-update) | async-done | bytes 196624
  491.4 4.1 fusion.70
  495.7 1.6 copy-done.10
  497.3 15.2 %fusion.99 = f32[4,768,3072]{2,1,0:T(8,128)} fusion(bf16[4,96,768]{2,1,0:T(8,128)(2,1)S(1)} %copy-done.20, bf16[4,96,3072]{2,1,0:T(8,128)(2,1)S(1)} %copy-done.10), kind=kOutput, calls=%fused_computation.168 | convolution fusion | flops 1811939328 | bytes 40697856 | tf_op jit(solution)/shard_map/ecd,ecf->edf/dot_general | solution.py:232
  513.6 17.7 %fusion.95 = f32[4,3072,768]{2,1,0:T(8,128)} fusion(bf16[4,96,768]{2,1,0:T(8,128)(2,1)S(1)} %copy-done.18, f32[4,96,3072]{2,1,0:T(8,128)} %get-tuple-element.751), kind=kOutput, calls=%fused_computation.164 | convolution fusion | flops 1822556160 | bytes 43057152 | tf_op jit(solution)/shard_map/ecf,ecd->efd/dot_general | solution.py:226
  532.3 10.7 fusion.55
  543.0 3.7 fusion.68
  546.8 39.7 %all-reduce = (f32[768]{0:T(1024)}, f32[12,32]{1,0:T(8,128)}, f32[768]{0:T(1024)}) all-reduce(f32[768]{0:T(1024)S(1)} %get-tuple-element.658, f32[12,32]{1,0:T(8,128)S(1)} %copy-done.35, f32[768]{0:T(1024)S(1)} %copy-done.45), channel_id=1, replica_groups=mesh['dp'=8,'seq'=4] {'dp','seq'}, use_global_device_ids=true, to_apply=%region_35.36 | all-reduce | flops 1920 | bytes 15360 | tf_op jit(solution)/shard_map/psum | solution.py:316
  587.4 7.9 reduce-scatter.13.cloned.1.call-done
  595.3 125.1 %reduce-scatter.11.cloned.1.call-done = f32[24,2304]{1,0:T(8,128)} async-done(((f32[768,2304]{1,0:T(8,128)}), f32[24,2304]{1,0:T(8,128)}) %reduce-scatter.11.cloned.1.call-update) | async-done | bytes 221200 | tf_op jit(solution)/shard_map/reduce_scatter | solution.py:320
  720.4 353.4 %reduce-scatter.15.cloned.1.call-done = f32[4,24,3072]{2,1,0:T(8,128)} async-done(((f32[4,768,3072]{2,1,0:T(8,128)}), f32[4,24,3072]{2,1,0:T(8,128)}) %reduce-scatter.15.cloned.1.call-update) | async-done | bytes 1179664 | tf_op jit(solution)/shard_map/reduce_scatter | solution.py:322
  1073.8 353.9 %reduce-scatter.17.cloned.1.call-done = f32[4,96,768]{2,1,0:T(8,128)} async-done(((f32[4,3072,768]{2,1,0:T(8,128)}), f32[4,96,768]{2,1,0:T(8,128)}) %reduce-scatter.17.cloned.1.call-update) | async-done | bytes 1179664 | tf_op jit(solution)/shard_map/reduce_scatter | solution.py:323
  (193 shorter events, 44.6 us)
Async XLA Ops:
  7.2 66.6 %copy-start.15 = (bf16[1,128,768]{2,1,0:T(8,128)(2,1)S(1)}, bf16[1,128,768]{2,1,0:T(8,128)(2,1)}, u32[]{:S(2)}) copy-start(bf16[1,128,768]{2,1,0:T(8,128)(2,1)} %param.28) | copy-start | bytes 589828
  7.2 66.6 %copy-start.40 = (f32[768]{0:T(1024)S(1)}, f32[768]{0:T(1024)}, u32[]{:S(2)}) copy-start(f32[768]{0:T(1024)} %param.34) | copy-start | bytes 9220
  7.2 66.6 %all-gather.6.cloned.1.call-start = ((), (), s32[]{:S(2)}) async-start(), calls=%async_computation.6 | async-start | bytes 3649536 | tf_op jit(solution)/shard_map/all_gather | solution.py:94
  7.9 121.6 %all-gather.8.cloned.1.call-start = ((), (), s32[]{:S(2)}) async-start(), calls=%async_computation.7 | async-start | bytes 1216512 | tf_op jit(solution)/shard_map/all_gather | solution.py:95
  8.7 247.4 %all-gather.12.cloned.1.call-start = ((), (), s32[]{:S(2)}) async-start(), calls=%async_computation.9 | async-start | bytes 19464192 | tf_op jit(solution)/shard_map/all_gather | solution.py:97
  9.4 372.3 %all-gather.10.cloned.1.call-start = ((), (), s32[]{:S(2)}) async-start(), calls=%async_computation.8 | async-start | bytes 19464192 | tf_op jit(solution)/shard_map/all_gather | solution.py:96
  10.0 453.9 %reduce-scatter.21.cloned.1.call-start = ((), (), s32[]{:S(2)}) async-start(), calls=%async_computation.15 | async-start | bytes 983040
  14.5 62.1 %copy-start.23 = (bf16[4,96,128]{2,1,0:T(8,128)(2,1)}, bf16[4,96,128]{2,1,0:T(8,128)(2,1)S(1)}, u32[]{:S(2)}) copy-start(bf16[4,96,128]{2,1,0:T(8,128)(2,1)S(1)} %copy.119) | copy-start | bytes 294916
  22.0 54.6 %copy-start.48 = (f32[4,96]{1,0:T(4,128)}, f32[4,96]{1,0:T(4,128)S(1)}, u32[]{:S(2)}) copy-start(f32[4,96]{1,0:T(4,128)S(1)} %convolution_bitcast_fusion) | copy-start | bytes 4612
  23.1 53.5 %copy-start.46 = (f32[128]{0:T(128)}, f32[128]{0:T(128)S(1)}, u32[]{:S(2)}) copy-start(f32[128]{0:T(128)S(1)} %add_rsqrt_fusion.1) | copy-start | bytes 1540
  76.5 20.5 %copy-start.19 = (bf16[12,32]{1,0:T(8,128)(2,1)S(1)}, bf16[12,32]{1,0:T(8,128)(2,1)}, u32[]{:S(2)}) copy-start(bf16[12,32]{1,0:T(8,128)(2,1)} %param.37) | copy-start | bytes 2308
  108.5 22.8 %copy-start.24 = (bf16[4,96,128]{2,1,0:T(8,128)(2,1)S(1)}, bf16[4,96,128]{2,1,0:T(8,128)(2,1)}, u32[]{:S(2)}) copy-start(bf16[4,96,128]{2,1,0:T(8,128)(2,1)} %copy-done.23) | copy-start | bytes 294916
  108.5 22.8 %copy-start.43 = (f32[768]{0:T(1024)S(1)}, f32[768]{0:T(1024)}, u32[]{:S(2)}) copy-start(f32[768]{0:T(1024)} %param.38) | copy-start | bytes 9220
  110.2 7.5 copy-start
  110.2 7.5 copy-start.4
  121.4 148.9 %copy-start.38 = (f32[12,128]{1,0:T(8,128)}, f32[12,128]{1,0:T(8,128)S(1)}, u32[]{:S(2)}) copy-start(f32[12,128]{1,0:T(8,128)S(1)} %get-tuple-element.1187) | copy-start | bytes 18436
  121.5 134.6 %copy-start.17 = (bf16[4,96,768]{2,1,0:T(8,128)(2,1)S(1)}, bf16[4,96,768]{2,1,0:T(8,128)(2,1)}, u32[]{:S(2)}) copy-start(bf16[4,96,768]{2,1,0:T(8,128)(2,1)} %fusion.47) | copy-start | bytes 1769476
  121.5 148.8 %copy-start.21 = (bf16[128,12,64]{0,2,1:T(8,128)(2,1)}, bf16[128,12,64]{0,2,1:T(8,128)(2,1)S(1)}, u32[]{:S(2)}) copy-start(bf16[128,12,64]{0,2,1:T(8,128)(2,1)S(1)} %convert_element_type.181) | copy-start | bytes 589828
  131.3 276.7 %copy-start.13 = (f32[128,768]{1,0:T(8,128)}, f32[128,768]{1,0:T(8,128)S(1)}, u32[]{:S(2)}) copy-start(f32[128,768]{1,0:T(8,128)S(1)} %get-tuple-element.749) | copy-start | bytes 1179652
  270.3 123.1 %copy-start.25 = (bf16[4,96,128]{2,1,0:T(8,128)(2,1)S(1)}, bf16[4,96,128]{2,1,0:T(8,128)(2,1)}, u32[]{:S(2)}) copy-start(bf16[4,96,128]{2,1,0:T(8,128)(2,1)} %copy-done.23) | copy-start | bytes 294916
  270.3 123.1 %copy-start.44 = (f32[768]{0:T(1024)S(1)}, f32[768]{0:T(1024)}, u32[]{:S(2)}) copy-start(f32[768]{0:T(1024)} %param.38) | copy-start | bytes 9220
  393.4 14.6 %copy-start.9 = (bf16[4,96,3072]{2,1,0:T(8,128)(2,1)}, bf16[4,96,3072]{2,1,0:T(8,128)(2,1)S(1)}, u32[]{:S(2)}) copy-start(bf16[4,96,3072]{2,1,0:T(8,128)(2,1)S(1)} %get-tuple-element.750) | copy-start | bytes 7077892
  418.3 5.6 copy-start.39
  423.9 2.5 copy-start.5
  426.3 1.7 copy-start.1
  426.3 2.4 copy-start.3
  428.7 3.5 copy-start.7
  439.9 6.7 copy-start.34
  439.9 4.8 copy-start.12
  439.9 4.8 copy-start.22
  442.3 48.0 %reduce-scatter.19.cloned.1.call-start = ((), (), s32[]{:S(2)}) async-start(), calls=%async_computation.14 | async-start | bytes 983040
  444.6 2.2 copy-start.8
  444.6 46.7 %copy-start.16 = (bf16[1,128,768]{2,1,0:T(8,128)(2,1)S(1)}, bf16[1,128,768]{2,1,0:T(8,128)(2,1)}, u32[]{:S(2)}) copy-start(bf16[1,128,768]{2,1,0:T(8,128)(2,1)} %param.28) | copy-start | bytes 589828
  444.6 46.7 %copy-start.41 = (f32[768]{0:T(1024)S(1)}, f32[768]{0:T(1024)}, u32[]{:S(2)}) copy-start(f32[768]{0:T(1024)} %param.34) | copy-start | bytes 9220
  444.7 46.7 %copy-start.47 = (f32[128]{0:T(128)S(1)}, f32[128]{0:T(128)}, u32[]{:S(2)}) copy-start(f32[128]{0:T(128)} %copy-done.46) | copy-start | bytes 1540
  444.7 150.6 %reduce-scatter.13.cloned.1.call-start = ((), (), s32[]{:S(2)}) async-start(), calls=%async_computation.11 | async-start | bytes 2433024 | tf_op jit(solution)/shard_map/reduce_scatter | solution.py:321
  446.6 273.8 %reduce-scatter.11.cloned.1.call-start = ((), (), s32[]{:S(2)}) async-start(), calls=%async_computation.10 | async-start | bytes 7299072 | tf_op jit(solution)/shard_map/reduce_scatter | solution.py:320
  446.9 48.7 %copy-start.31 = (bf16[128,12,64]{0,2,1:T(8,128)(2,1)}, bf16[128,12,64]{0,2,1:T(8,128)(2,1)S(1)}, u32[]{:S(2)}) copy-start(bf16[128,12,64]{0,2,1:T(8,128)(2,1)S(1)} %convert_element_type.204) | copy-start | bytes 589828
  464.9 30.6 %copy-start.27 = (bf16[128,768]{0,1:T(8,128)(2,1)}, bf16[128,768]{0,1:T(8,128)(2,1)S(1)}, u32[]{:S(2)}) copy-start(bf16[128,768]{0,1:T(8,128)(2,1)S(1)} %copy.128) | copy-start | bytes 589828
  491.4 4.2 copy-start.29
  495.6 1.8 copy-start.20
  495.6 578.2 %reduce-scatter.15.cloned.1.call-start = ((), (), s32[]{:S(2)}) async-start(), calls=%async_computation.12 | async-start | bytes 38928384 | tf_op jit(solution)/shard_map/reduce_scatter | solution.py:322
  512.5 915.2 %reduce-scatter.17.cloned.1.call-start = ((), (), s32[]{:S(2)}) async-start(), calls=%async_computation.13 | async-start | bytes 38928384 | tf_op jit(solution)/shard_map/reduce_scatter | solution.py:323
  532.3 10.7 copy-start.28
  532.3 10.7 copy-start.30
  532.3 10.7 copy-start.32
  543.0 3.8 copy-start.35
  543.0 3.7 copy-start.45
  (12 other events, 14.4 us)
Sparse Core Ops, SparseCore 0:
  10.9 62.8 all-gather.5
  76.7 52.8 all-gather.7
  132.5 123.5 all-gather.11
  258.9 122.7 all-gather.9
  442.4 21.4 reduce-scatter.20
  467.0 23.2 reduce-scatter.18
  496.1 99.1 reduce-scatter.12
  602.5 117.8 reduce-scatter.10
  727.4 346.3 reduce-scatter.14
  1081.8 345.9 reduce-scatter.16
where the time goes:
time: 1440 us; the launch traced here: 1430 us
  waiting for transfers between devices  1180 us (82%)
  matrix products  125 us (9%)
  blocking collectives  63 us (4%)
  local copies, waits for them, and re-layouts  31.1 us (2%)
  other arithmetic  20 us (1%)
  between operations  14.8 us (1%)
    reduce_scatter x1, waiting for transfers between devices, body(): lax.psum_scatter(grad_w_out, ('dp', 'seq'), scatter_dimension=1, tiled=True)  354 us
    reduce_scatter x1, waiting for transfers between devices, body(): lax.psum_scatter(grad_w_in, ('dp', 'seq'), scatter_dimension=1, tiled=True)  353 us
    reduce_scatter x1, waiting for transfers between devices, body(): lax.psum_scatter(grad_w_qkv, ('dp', 'seq'), scatter_dimension=0, tiled=True)  125 us
    all_gather x1, waiting for transfers between devices, body(): lax.all_gather(w_expert_out, ('dp', 'seq'), axis=1, tiled=True)  124 us
    all_gather x1, waiting for transfers between devices, body(): lax.all_gather(w_expert_in, ('dp', 'seq'), axis=1, tiled=True)  111 us
    all_gather x1, waiting for transfers between devices, body(): lax.all_gather(w_qkv, ('dp', 'seq'), axis=0, tiled=True)  48.6 us
    unnamed x12, waiting for transfers between devices  45 us
    psum x1, blocking collectives, body(): lax.psum((grad_table, grad_gain_one, grad_gain_two), ('dp', 'seq'))  39.7 us
  transfers between devices with their start and end apart: 10, of which 10 were waited for; matrix products, arithmetic and copies ran while one was open for 8% of the time, Pallas kernels for 0%

commit v1 on v0

--- a/solution.py
+++ b/solution.py
@@ -314,7 +314,7 @@
     grad_input_norm, grad_gain_one = norm_back(grad_normed_one, scaled_one, factor_one, gain_one)
     grad_inputs = grad_hidden + grad_input_norm
     table_total, gain_one_total, gain_two_total = lax.psum(
-        (grad_table, grad_gain_one, grad_gain_two), ("dp", "seq")
+        lax.psum((grad_table, grad_gain_one, grad_gain_two), "seq"), "dp"
     )
     shares = (
         lax.psum_scatter(grad_w_qkv, ("dp", "seq"), scatter_dimension=0, tiled=True),

time: 1440 us -> 1440 us (level)
    psum x1 -> x2, blocking collectives: 39.7 us -> 48.6 us  [the longest x1 37.7 us: body(): lax.psum(lax.psum((grad_table, grad_gain_one, grad_gain_two), 'seq'), 'dp')]
  transfers between devices with their start and end apart: 10 -> 10, of which waited for: 10 -> 9; matrix products, arithmetic and copies ran while one was open for 8% -> 8% of each run, Pallas kernels for 0% -> 0%
where the time goes in v1:
time: 1440 us; the launch traced here: 1430 us
  waiting for transfers between devices  1170 us (81%)
  matrix products  125 us (9%)
  blocking collectives  71.9 us (5%)
  local copies, waits for them, and re-layouts  31.1 us (2%)
  other arithmetic  19.9 us (1%)
  between operations  14.8 us (1%)
    reduce_scatter x1, waiting for transfers between devices, body(): lax.psum_scatter(grad_w_out, ('dp', 'seq'), scatter_dimension=1, tiled=True)  354 us
    reduce_scatter x1, waiting for transfers between devices, body(): lax.psum_scatter(grad_w_in, ('dp', 'seq'), scatter_dimension=1, tiled=True)  353 us
    reduce_scatter x1, waiting for transfers between devices, body(): lax.psum_scatter(grad_w_qkv, ('dp', 'seq'), scatter_dimension=0, tiled=True)  124 us
    all_gather x1, waiting for transfers between devices, body(): lax.all_gather(w_expert_out, ('dp', 'seq'), axis=1, tiled=True)  124 us
    all_gather x1, waiting for transfers between devices, body(): lax.all_gather(w_expert_in, ('dp', 'seq'), axis=1, tiled=True)  111 us
    all_gather x1, waiting for transfers between devices, body(): lax.all_gather(w_qkv, ('dp', 'seq'), axis=0, tiled=True)  48.6 us
    unnamed x12, waiting for transfers between devices  45 us
    psum x1, blocking collectives, body(): lax.psum(lax.psum((grad_table, grad_gain_one, grad_gain_two), 'seq'), 'dp')  37.7 us
  transfers between devices with their start and end apart: 10, of which 9 were waited for; matrix products, arithmetic and copies ran while one was open for 8% of the time, Pallas kernels for 0%

profile of v1, /device:TPU:0, one launch (start us, length us, event | category | flops | bytes accessed | tf_op | source)
XLA Modules:
  0.0 1434.3 jit_solution(13954265193933379)
XLA Ops:
  15.2 5.9 all-gather
  23.1 2.0 fusion.47
  25.1 48.6 %all-gather.6.cloned.1.call-done = bf16[768,2304]{1,0:T(8,128)(2,1)} async-done(((bf16[24,2304]{1,0:T(8,128)(2,1)}), bf16[768,2304]{1,0:T(8,128)(2,1)}) %all-gather.6.cloned.1.call-update) | async-done | bytes 3538960 | tf_op jit(solution)/shard_map/all_gather | solution.py:94
  73.8 2.7 convolution_convert_fusion
  76.6 8.6 all_gather.27
  86.5 8.7 all_gather.28
  97.0 10.8 while.44
  98.5 4.7 conditional.20
  101.4 1.8 copy.138
  104.1 2.0 fusion.162
  108.5 12.9 while.45
  110.2 6.7 conditional.21
  110.2 1.7 convert_reduce_fusion.4
  113.2 3.7 copy.139
  117.7 3.5 fusion.167
  121.5 8.0 all-gather.8.cloned.1.call-done
  129.6 1.7 multiply_reduce_fusion.3
  132.5 123.6 %all-gather.12.cloned.1.call-done = bf16[4,3072,768]{2,1,0:T(8,128)(2,1)} async-done(((bf16[4,96,768]{2,1,0:T(8,128)(2,1)}), bf16[4,3072,768]{2,1,0:T(8,128)(2,1)}) %all-gather.12.cloned.1.call-update) | async-done | bytes 18874384 | tf_op jit(solution)/shard_map/all_gather | solution.py:97
  256.1 14.2 fusion.98
  270.3 111.4 %all-gather.10.cloned.1.call-done = bf16[4,768,3072]{2,1,0:T(8,128)(2,1)} async-done(((bf16[4,24,3072]{2,1,0:T(8,128)(2,1)}), bf16[4,768,3072]{2,1,0:T(8,128)(2,1)}) %all-gather.10.cloned.1.call-update) | async-done | bytes 18874384 | tf_op jit(solution)/shard_map/all_gather | solution.py:96
  381.7 11.7 fusion.46
  393.4 14.6 %multiply_reduce_fusion = (f32[768]{0:T(1024)}, f32[128]{0:T(128)S(1)}, f32[128,768]{1,0:T(8,128)}) fusion(f32[128,768]{1,0:T(8,128)S(1)} %get-tuple-element.752, f32[128]{0:T(128)S(1)} %add_rsqrt_fusion, f32[768]{0:T(1024)S(1)} %copy-done.44, bf16[4,96,128]{2,1,0:T(8,128)(2,1)S(1)} %copy-done.25, bf16[4,96,3072]{2,1,0:T(8,128)(2,1)S(1)} %get-tuple-element.753, ...), kind=kOutput, calls=%fused_computation.122 | convolution fusion | flops 1888320640 | bytes 22125568 | tf_op jit(solution)/shard_map/ect,ecd->td/dot_general | solution.py:236
  409.9 1.8 convolution_convert_fusion.3
  416.3 23.3 %while.46 = (s32[]{:T(128)}, f32[128,12,64]{0,2,1:T(8,128)}, bf16[512,768]{0,1:T(8,128)(2,1)}, bf16[512,768]{0,1:T(8,128)(2,1)}, f32[12,32]{1,0:T(8,128)S(1)}, /...) while((s32[]{:T(128)}, f32[128,12,64]{0,2,1:T(8,128)}, ...), condition=%wide.region_30.31_spmd.clone.clone, body=%wide.region_21.30_spmd.sunk.clone.clone.sunk | while | flops 628818944 | bytes 50517476 | solution.py:289
  418.0 4.7 conditional.22
  420.9 1.8 copy.135
  423.6 2.4 exponential_select_fusion.2
  426.0 1.7 multiply_convert_fusion.7
  429.7 2.2 fusion.180
  431.9 7.6 conditional.23
  431.9 3.0 copy.106
  436.6 2.9 fusion.15
  439.6 2.3 copy.127
  442.0 2.3 copy.125
  444.4 1.8 fusion.77
  446.6 17.0 %reduce-scatter.21.cloned.1.call-done = bf16[128,768]{1,0:T(8,128)(2,1)} async-done(((bf16[512,768]{1,0:T(8,128)(2,1)}), bf16[128,768]{1,0:T(8,128)(2,1)}) %reduce-scatter.21.cloned.1.call-update) | async-done | bytes 196624
  464.6 25.3 %reduce-scatter.19.cloned.1.call-done = bf16[128,768]{1,0:T(8,128)(2,1)} async-done(((bf16[512,768]{1,0:T(8,128)(2,1)}), bf16[128,768]{1,0:T(8,128)(2,1)}) %reduce-scatter.19.cloned.1.call-update) | async-done | bytes 196624
  491.1 4.2 fusion.70
  495.3 1.6 copy-done.10
  497.0 15.2 %fusion.99 = f32[4,768,3072]{2,1,0:T(8,128)} fusion(bf16[4,96,768]{2,1,0:T(8,128)(2,1)S(1)} %copy-done.20, bf16[4,96,3072]{2,1,0:T(8,128)(2,1)S(1)} %copy-done.10), kind=kOutput, calls=%fused_computation.168 | convolution fusion | flops 1811939328 | bytes 40697856 | tf_op jit(solution)/shard_map/ecd,ecf->edf/dot_general | solution.py:232
  513.3 17.7 %fusion.95 = f32[4,3072,768]{2,1,0:T(8,128)} fusion(bf16[4,96,768]{2,1,0:T(8,128)(2,1)S(1)} %copy-done.18, f32[4,96,3072]{2,1,0:T(8,128)} %get-tuple-element.754), kind=kOutput, calls=%fused_computation.164 | convolution fusion | flops 1822556160 | bytes 43057152 | tf_op jit(solution)/shard_map/ecf,ecd->efd/dot_general | solution.py:226
  532.0 10.7 fusion.55
  542.7 3.7 fusion.68
  546.4 10.9 all-reduce.1
  557.4 37.7 %all-reduce = (f32[768]{0:T(1024)}, f32[12,32]{1,0:T(8,128)}, f32[768]{0:T(1024)}) all-reduce(f32[768]{0:T(1024)S(1)} %get-tuple-element.737, f32[12,32]{1,0:T(8,128)S(1)} %get-tuple-element.738, f32[768]{0:T(1024)S(1)} %get-tuple-element.739), channel_id=1, replica_groups=mesh['dp'=8,'seq'=4] {'dp'}, use_global_device_ids=true, to_apply=%region_36.37 | all-reduce | flops 1920 | bytes 15360 | tf_op jit(solution)/shard_map/psum | solution.py:316
  596.0 124.4 %reduce-scatter.11.cloned.1.call-done = f32[24,2304]{1,0:T(8,128)} async-done(((f32[768,2304]{1,0:T(8,128)}), f32[24,2304]{1,0:T(8,128)}) %reduce-scatter.11.cloned.1.call-update) | async-done | bytes 221200 | tf_op jit(solution)/shard_map/reduce_scatter | solution.py:320
  720.3 353.0 %reduce-scatter.15.cloned.1.call-done = f32[4,24,3072]{2,1,0:T(8,128)} async-done(((f32[4,768,3072]{2,1,0:T(8,128)}), f32[4,24,3072]{2,1,0:T(8,128)}) %reduce-scatter.15.cloned.1.call-update) | async-done | bytes 1179664 | tf_op jit(solution)/shard_map/reduce_scatter | solution.py:322
  1073.3 353.9 %reduce-scatter.17.cloned.1.call-done = f32[4,96,768]{2,1,0:T(8,128)} async-done(((f32[4,3072,768]{2,1,0:T(8,128)}), f32[4,96,768]{2,1,0:T(8,128)}) %reduce-scatter.17.cloned.1.call-update) | async-done | bytes 1179664 | tf_op jit(solution)/shard_map/reduce_scatter | solution.py:323
  (194 shorter events, 44.5 us)
Async XLA Ops:
  7.2 66.6 %copy-start.15 = (bf16[1,128,768]{2,1,0:T(8,128)(2,1)S(1)}, bf16[1,128,768]{2,1,0:T(8,128)(2,1)}, u32[]{:S(2)}) copy-start(bf16[1,128,768]{2,1,0:T(8,128)(2,1)} %param.28) | copy-start | bytes 589828
  7.2 66.6 %copy-start.40 = (f32[768]{0:T(1024)S(1)}, f32[768]{0:T(1024)}, u32[]{:S(2)}) copy-start(f32[768]{0:T(1024)} %param.34) | copy-start | bytes 9220
  7.2 66.6 %all-gather.6.cloned.1.call-start = ((), (), s32[]{:S(2)}) async-start(), calls=%async_computation.6 | async-start | bytes 3649536 | tf_op jit(solution)/shard_map/all_gather | solution.py:94
  7.9 121.6 %all-gather.8.cloned.1.call-start = ((), (), s32[]{:S(2)}) async-start(), calls=%async_computation.7 | async-start | bytes 1216512 | tf_op jit(solution)/shard_map/all_gather | solution.py:95
  8.7 247.4 %all-gather.12.cloned.1.call-start = ((), (), s32[]{:S(2)}) async-start(), calls=%async_computation.9 | async-start | bytes 19464192 | tf_op jit(solution)/shard_map/all_gather | solution.py:97
  9.4 372.3 %all-gather.10.cloned.1.call-start = ((), (), s32[]{:S(2)}) async-start(), calls=%async_computation.8 | async-start | bytes 19464192 | tf_op jit(solution)/shard_map/all_gather | solution.py:96
  10.0 453.5 %reduce-scatter.21.cloned.1.call-start = ((), (), s32[]{:S(2)}) async-start(), calls=%async_computation.15 | async-start | bytes 983040
  14.5 62.1 %copy-start.23 = (bf16[4,96,128]{2,1,0:T(8,128)(2,1)}, bf16[4,96,128]{2,1,0:T(8,128)(2,1)S(1)}, u32[]{:S(2)}) copy-start(bf16[4,96,128]{2,1,0:T(8,128)(2,1)S(1)} %copy.119) | copy-start | bytes 294916
  22.0 54.6 %copy-start.48 = (f32[4,96]{1,0:T(4,128)}, f32[4,96]{1,0:T(4,128)S(1)}, u32[]{:S(2)}) copy-start(f32[4,96]{1,0:T(4,128)S(1)} %convolution_bitcast_fusion) | copy-start | bytes 4612
  23.1 53.5 %copy-start.46 = (f32[128]{0:T(128)}, f32[128]{0:T(128)S(1)}, u32[]{:S(2)}) copy-start(f32[128]{0:T(128)S(1)} %add_rsqrt_fusion.1) | copy-start | bytes 1540
  76.5 20.5 %copy-start.19 = (bf16[12,32]{1,0:T(8,128)(2,1)S(1)}, bf16[12,32]{1,0:T(8,128)(2,1)}, u32[]{:S(2)}) copy-start(bf16[12,32]{1,0:T(8,128)(2,1)} %param.37) | copy-start | bytes 2308
  108.5 22.8 %copy-start.24 = (bf16[4,96,128]{2,1,0:T(8,128)(2,1)S(1)}, bf16[4,96,128]{2,1,0:T(8,128)(2,1)}, u32[]{:S(2)}) copy-start(bf16[4,96,128]{2,1,0:T(8,128)(2,1)} %copy-done.23) | copy-start | bytes 294916
  108.5 22.8 %copy-start.43 = (f32[768]{0:T(1024)S(1)}, f32[768]{0:T(1024)}, u32[]{:S(2)}) copy-start(f32[768]{0:T(1024)} %param.38) | copy-start | bytes 9220
  110.2 7.5 copy-start
  110.2 7.5 copy-start.4
  121.5 148.9 %copy-start.38 = (f32[12,128]{1,0:T(8,128)}, f32[12,128]{1,0:T(8,128)S(1)}, u32[]{:S(2)}) copy-start(f32[12,128]{1,0:T(8,128)S(1)} %get-tuple-element.1190) | copy-start | bytes 18436
  121.5 134.6 %copy-start.17 = (bf16[4,96,768]{2,1,0:T(8,128)(2,1)S(1)}, bf16[4,96,768]{2,1,0:T(8,128)(2,1)}, u32[]{:S(2)}) copy-start(bf16[4,96,768]{2,1,0:T(8,128)(2,1)} %fusion.47) | copy-start | bytes 1769476
  121.5 148.8 %copy-start.21 = (bf16[128,12,64]{0,2,1:T(8,128)(2,1)}, bf16[128,12,64]{0,2,1:T(8,128)(2,1)S(1)}, u32[]{:S(2)}) copy-start(bf16[128,12,64]{0,2,1:T(8,128)(2,1)S(1)} %convert_element_type.181) | copy-start | bytes 589828
  131.3 276.7 %copy-start.13 = (f32[128,768]{1,0:T(8,128)}, f32[128,768]{1,0:T(8,128)S(1)}, u32[]{:S(2)}) copy-start(f32[128,768]{1,0:T(8,128)S(1)} %get-tuple-element.752) | copy-start | bytes 1179652
  270.3 123.0 %copy-start.25 = (bf16[4,96,128]{2,1,0:T(8,128)(2,1)S(1)}, bf16[4,96,128]{2,1,0:T(8,128)(2,1)}, u32[]{:S(2)}) copy-start(bf16[4,96,128]{2,1,0:T(8,128)(2,1)} %copy-done.23) | copy-start | bytes 294916
  270.3 123.0 %copy-start.44 = (f32[768]{0:T(1024)S(1)}, f32[768]{0:T(1024)}, u32[]{:S(2)}) copy-start(f32[768]{0:T(1024)} %param.38) | copy-start | bytes 9220
  393.4 14.6 %copy-start.9 = (bf16[4,96,3072]{2,1,0:T(8,128)(2,1)}, bf16[4,96,3072]{2,1,0:T(8,128)(2,1)S(1)}, u32[]{:S(2)}) copy-start(bf16[4,96,3072]{2,1,0:T(8,128)(2,1)S(1)} %get-tuple-element.753) | copy-start | bytes 7077892
  418.0 5.6 copy-start.39
  423.6 2.5 copy-start.5
  426.0 1.7 copy-start.1
  426.0 2.4 copy-start.3
  428.4 3.5 copy-start.7
  439.5 6.7 copy-start.34
  439.6 4.8 copy-start.12
  439.6 4.8 copy-start.22
  441.9 48.0 %reduce-scatter.19.cloned.1.call-start = ((), (), s32[]{:S(2)}) async-start(), calls=%async_computation.14 | async-start | bytes 983040
  444.3 2.2 copy-start.8
  444.3 46.7 %copy-start.16 = (bf16[1,128,768]{2,1,0:T(8,128)(2,1)S(1)}, bf16[1,128,768]{2,1,0:T(8,128)(2,1)}, u32[]{:S(2)}) copy-start(bf16[1,128,768]{2,1,0:T(8,128)(2,1)} %param.28) | copy-start | bytes 589828
  444.3 46.7 %copy-start.41 = (f32[768]{0:T(1024)S(1)}, f32[768]{0:T(1024)}, u32[]{:S(2)}) copy-start(f32[768]{0:T(1024)} %param.34) | copy-start | bytes 9220
  444.3 46.7 %copy-start.47 = (f32[128]{0:T(128)S(1)}, f32[128]{0:T(128)}, u32[]{:S(2)}) copy-start(f32[128]{0:T(128)} %copy-done.46) | copy-start | bytes 1540
  444.3 151.6 %reduce-scatter.13.cloned.1.call-start = ((), (), s32[]{:S(2)}) async-start(), calls=%async_computation.11 | async-start | bytes 2433024 | tf_op jit(solution)/shard_map/reduce_scatter | solution.py:321
  446.3 274.1 %reduce-scatter.11.cloned.1.call-start = ((), (), s32[]{:S(2)}) async-start(), calls=%async_computation.10 | async-start | bytes 7299072 | tf_op jit(solution)/shard_map/reduce_scatter | solution.py:320
  446.5 48.7 %copy-start.31 = (bf16[128,12,64]{0,2,1:T(8,128)(2,1)}, bf16[128,12,64]{0,2,1:T(8,128)(2,1)S(1)}, u32[]{:S(2)}) copy-start(bf16[128,12,64]{0,2,1:T(8,128)(2,1)S(1)} %convert_element_type.204) | copy-start | bytes 589828
  464.6 30.6 %copy-start.27 = (bf16[128,768]{0,1:T(8,128)(2,1)}, bf16[128,768]{0,1:T(8,128)(2,1)S(1)}, u32[]{:S(2)}) copy-start(bf16[128,768]{0,1:T(8,128)(2,1)S(1)} %copy.128) | copy-start | bytes 589828
  491.0 4.2 copy-start.29
  495.3 1.8 copy-start.20
  495.3 578.1 %reduce-scatter.15.cloned.1.call-start = ((), (), s32[]{:S(2)}) async-start(), calls=%async_computation.12 | async-start | bytes 38928384 | tf_op jit(solution)/shard_map/reduce_scatter | solution.py:322
  512.2 915.1 %reduce-scatter.17.cloned.1.call-start = ((), (), s32[]{:S(2)}) async-start(), calls=%async_computation.13 | async-start | bytes 38928384 | tf_op jit(solution)/shard_map/reduce_scatter | solution.py:323
  532.0 10.7 copy-start.28
  532.0 10.7 copy-start.30
  532.0 10.7 copy-start.32
  542.6 3.8 copy-start.35
  542.7 3.7 copy-start.45
  (12 other events, 14.2 us)
Sparse Core Ops, SparseCore 0:
  10.9 62.8 all-gather.5
  76.7 52.8 all-gather.7
  132.5 123.5 all-gather.11
  258.9 122.7 all-gather.9
  442.1 21.4 reduce-scatter.20
  466.7 23.2 reduce-scatter.18
  495.8 99.1 reduce-scatter.12
  602.2 118.0 reduce-scatter.10
  727.3 345.9 reduce-scatter.14
  1081.3 345.9 reduce-scatter.16
